TPU v7x, 1024 devices: a whole 8x8x8 slice. The times are simulated.
1024 devices in a mesh: seq: 32 (over y, x_hi, core), head: 32 (over z, x_lo).
Axes of the slice: x: 8 (x_hi: 2, x_lo: 4; x = x_hi * 4 + x_lo), y: 8, z: 8, core: 2. Of those that a mesh axis runs over, the one named last changes fastest.
Arguments:
- main_query: bfloat16 [4096, 73728], P('seq', 'head'), may hold values from -18 to 18
- latent: bfloat16 [8192, 576], P('seq'), may hold values from -6 to 6
- main_outside: float32 [4096, 128], P('seq', 'head'), may hold values from 5 to 11
- index_query: bfloat16 [4096, 8192], P('seq', 'head'), may hold values from -6 to 6
- index_weights: float32 [4096, 64], P('seq', 'head'), may hold values from -2.4 to 2.4
- index_keys: bfloat16 [8192, 128], P('seq'), may hold values from -6 to 6
- index_outside: float32 [4096], P('seq'), may hold values from 6 to 10
- query_pos: int32 [4096], P('seq'), may hold values from 1 to 16383, as said below
- key_pos: int32 [8192], P('seq'), may hold values from 0 to 16383, as said below
Outputs:
- grad_index_query: bfloat16 [4096, 8192], P('seq', 'head')
- grad_index_weights: float32 [4096, 64], P('seq', 'head')
- grad_index_keys: float32 [8192, 128], P('seq')
Inputs may be any that keep to these rules, and one draw needn't show every extreme that they name: `key_pos`: key j of block b stands at 2 * 256 * b + 2 * j or one more; key 0 of a block at 2 * 256 * b exactly. `query_pos`: queries of block b stand at 2 * 256 * b + 1 to 2 * 256 * b + 2 * 256 - 1.
All inputs are finite; a program needn't handle non-finite values.
Results may differ from a plain program's by a relative error of at most 0.00205.
Values may be sent and summed in bfloat16 or wider, within the bound.
A program may use at most 32 MiB of HBM per device.

v0:
```python
import jax
import jax.numpy as jnp
from jax import lax
from jax.sharding import PartitionSpec as P

IDIM = 128
KB = 256
STEPS = 4


NEGATIVE = -1e30
SCORE_SCALE = 192.0 ** (-0.5)


def passed_along(block, axis, distance):
    devices = range(lax.axis_size(axis))
    route = [(i - distance, i) for i in devices if i - distance in devices]
    return lax.ppermute(block, axis, route)


def head_mass(scores, visible, outside):
    masked = jnp.where(visible[None], scores, NEGATIVE)
    highest = jnp.maximum(jnp.max(masked, axis=2), outside.T)
    expo = jnp.exp(masked - highest[:, :, None])
    total = jnp.sum(expo, axis=2) + jnp.exp(outside.T - highest)
    return jnp.sum(expo / total[:, :, None], axis=0)


def score_grad(mass, index_score, visible, outside):
    target = mass / jnp.sum(mass, axis=1, keepdims=True)
    masked = jnp.where(visible, index_score, NEGATIVE)
    highest = jnp.maximum(jnp.max(masked, axis=1), outside)
    expo = jnp.exp(masked - highest[:, None])
    total = jnp.sum(expo, axis=1) + jnp.exp(outside - highest)
    return (expo / total[:, None] - target) * (STEPS * KB)


def shards(
    main_query,
    latent,
    main_outside,
    index_query,
    index_weights,
    index_keys,
    index_outside,
    query_pos,
    key_pos,
):
    query_rows = main_query.shape[0]
    block_keys = latent.shape[0]
    width = latent.shape[1]
    local_heads = main_outside.shape[1]
    local_index = index_weights.shape[1]
    index_width = index_keys.shape[1]
    window = STEPS * block_keys
    factor = IDIM ** (-0.5)
    position = lax.axis_index("seq")
    latent_parts = []
    index_parts = []
    for distance in range(STEPS - 1, 0, -1):
        latent_parts.append(passed_along(latent, "seq", distance))
        index_parts.append(passed_along(index_keys, "seq", distance))
    latent_window = jnp.concatenate(latent_parts + [latent], 0)
    key_window = jnp.concatenate(index_parts + [index_keys], 0)
    slot_block = jnp.arange(window, dtype=jnp.int32) // block_keys
    lagging = STEPS - 1 - slot_block
    places_full = jnp.concatenate([jnp.zeros((window - block_keys,), jnp.int32), key_pos], 0)
    causal = (slot_block < STEPS - 1)[None, :] | (places_full[None, :] <= query_pos[:, None])
    visible = (position >= lagging)[None, :] & causal
    queries = main_query.reshape(query_rows, local_heads, width)
    scores = (
        jnp.einsum("qhc,wc->hqw", queries, latent_window, preferred_element_type=jnp.float32)
        * SCORE_SCALE
    )
    mass_part = head_mass(scores, visible, main_outside)
    index_rows = index_query.reshape(query_rows, local_index, index_width)
    activity = (
        jnp.einsum("qjd,wd->jqw", index_rows, key_window, preferred_element_type=jnp.float32)
        * factor
    )
    rectified = jnp.maximum(activity, 0.0)
    index_part = jnp.einsum("qj,jqw->qw", index_weights, rectified)
    mass, index_score = lax.psum((mass_part, index_part), "head")
    dscore = score_grad(mass, index_score, visible, index_outside)
    gated = dscore[None] * index_weights.T[:, :, None] * (activity > 0).astype(jnp.float32)
    key_wide = key_window.astype(jnp.float32)
    rows_wide = index_rows.astype(jnp.float32)
    grad_query = (
        jnp.einsum("jqw,wd->qjd", gated, key_wide, precision=lax.Precision.HIGHEST) * factor
    )
    grad_query = grad_query.astype(jnp.bfloat16).reshape(query_rows, local_index * index_width)
    grad_weight = jnp.einsum("qw,jqw->qj", dscore, rectified)
    grad_window = (
        jnp.einsum("jqw,qjd->wd", gated, rows_wide, precision=lax.Precision.HIGHEST) * factor
    )
    grad_parts = grad_window.reshape(STEPS, block_keys, index_width)
    grad_total = grad_parts[STEPS - 1]
    for distance in range(1, STEPS):
        grad_total = grad_total + passed_along(grad_parts[STEPS - 1 - distance], "seq", -distance)
    grad_keys = lax.psum(grad_total, "head")
    return (grad_query, grad_weight, grad_keys)


def solution(mesh):
    in_specs = (
        P("seq", "head"),
        P("seq", None),
        P("seq", "head"),
        P("seq", "head"),
        P("seq", "head"),
        P("seq", None),
        P("seq"),
        P("seq"),
        P("seq"),
    )
    out_specs = (P("seq", "head"), P("seq", "head"), P("seq", None))
    return jax.shard_map(shards, mesh=mesh, in_specs=in_specs, out_specs=out_specs, check_vma=False)
```

profile of v0, /device:TPU:14, one launch (start us, length us, event | category | flops | bytes accessed | tf_op | source)
XLA Modules:
  0.0 704.9 jit_solution(6095280414498491521)
XLA Ops:
  7.2 5.6 collective-permute-start.3
  12.9 4.7 collective-permute-start.4
  17.6 3.6 collective-permute-start
  21.2 6.2 collective-permute-start.1
  27.4 1.9 collective-permute-start.2
  29.3 0.7 concatenate.10
  30.0 1.5 or_and_fusion
  31.5 1.4 copy.19
  32.9 4.9 collective-permute-start.5
  37.9 1.2 broadcast_compare_fusion
  39.1 0.9 multiply_reduce_fusion.1
  40.0 5.9 collective-permute-done.5
  46.0 1.0 fusion.39
  47.0 0.3 fusion
  47.4 1.2 divide_reduce_fusion
  48.6 330.3 %all-reduce.7.cloned.1.call-done = (f32[128,1024]{0,1:T(8,128)}, f32[128,1024]{0,1:T(8,128)}) async-done(((f32[128,1024]{0,1:T(8,128)}, f32[128,1024]{0,1:T(8,128)}), (f32[128,1024]{0,1:T(8,128)}, f32[128,1024]{0,1:T(8,128)})) %all-reduce.7.cloned.1.call-update) | async-done | bytes 1048592 | tf_op jit(solution)/shard_map/psum | solution.py:83
  378.9 1.8 fusion.18
  380.7 1.8 fusion.17
  382.5 1.2 reduce_sum.39
  383.7 2.0 subtract_multiply_fusion
  385.7 0.7 fusion.1
  386.5 1.9 collective-permute-start.6
  388.4 4.7 collective-permute-start.7
  393.1 1.3 collective-permute-start.8
  394.4 0.7 fusion.8
  395.1 0.7 copy.23
  395.8 6.7 collective-permute-done.7
  402.6 1.7 collective-permute-done.8
  404.3 0.7 fusion.20
  405.0 0.7 multiply_reduce_fusion
  405.7 290.8 %all-reduce.5.cloned.1.call-done = f32[256,128]{1,0:T(8,128)} async-done(((f32[256,128]{1,0:T(8,128)}), f32[256,128]{1,0:T(8,128)}) %all-reduce.5.cloned.1.call-update) | async-done | bytes 131088 | tf_op jit(solution)/shard_map/psum | solution.py:100
  696.5 1.6 copy.57
  (30 shorter events, 0.2 us)
Async XLA Ops:
  7.2 30.7 %copy-start = (bf16[128,256]{1,0:T(8,128)(2,1)S(1)}, bf16[128,256]{1,0:T(8,128)(2,1)}, u32[]{:S(2)}) copy-start(bf16[128,256]{1,0:T(8,128)(2,1)} %param.12) | copy-start | bytes 196612
  7.2 371.7 %all-reduce.7.cloned.1.call-start = ((), (), s32[]{:S(2)}) async-start(), calls=%async_computation.1 | async-start | bytes 2097152 | tf_op jit(solution)/shard_map/psum | solution.py:83
  7.2 32.8 %collective-permute-start.3 = (bf16[256,576]{0,1:T(8,128)(2,1)}, bf16[256,576]{0,1:T(8,128)(2,1)S(1)}, u32[]{:S(2)}, u32[]{:S(2)}) collective-permute-start(bf16[256,576]{0,1:T(8,128)(2,1)} %param.10), channel_id=1, source_target_pairs={{0,96},{32,128},{64,160},{96,192},{128,224},{160,256},{192,288},{2... | collective-permute-start | bytes 884744 | tf_op jit(solution)/shard_map/ppermute | solution.py:18
  12.9 27.2 %collective-permute-start.4 = (bf16[256,576]{0,1:T(8,128)(2,1)}, bf16[256,576]{0,1:T(8,128)(2,1)S(1)}, u32[]{:S(2)}, u32[]{:S(2)}) collective-permute-start(bf16[256,576]{0,1:T(8,128)(2,1)} %param.10), channel_id=1, source_target_pairs={{0,64},{32,96},{64,128},{96,160},{128,192},{160,224},{192,256},{22... | collective-permute-start | bytes 884744 | tf_op jit(solution)/shard_map/ppermute | solution.py:18
  17.6 15.4 %collective-permute-start = (bf16[256,128]{1,0:T(8,128)(2,1)}, bf16[256,128]{1,0:T(8,128)(2,1)S(1)}, u32[]{:S(2)}, u32[]{:S(2)}) collective-permute-start(bf16[256,128]{1,0:T(8,128)(2,1)} %param.14), channel_id=1, source_target_pairs={{0,96},{32,128},{64,160},{96,192},{128,224},{160,256},{192,288},{2... | collective-permute-start | bytes 196616 | tf_op jit(solution)/shard_map/ppermute | solution.py:18
  21.2 16.7 %collective-permute-start.1 = (bf16[256,128]{1,0:T(8,128)(2,1)}, bf16[256,128]{1,0:T(8,128)(2,1)S(1)}, u32[]{:S(2)}, u32[]{:S(2)}) collective-permute-start(bf16[256,128]{1,0:T(8,128)(2,1)} %param.14), channel_id=1, source_target_pairs={{0,64},{32,96},{64,128},{96,160},{128,192},{160,224},{192,256},{22... | collective-permute-start | bytes 196616 | tf_op jit(solution)/shard_map/ppermute | solution.py:18
  27.4 10.5 %collective-permute-start.2 = (bf16[256,128]{1,0:T(8,128)(2,1)}, bf16[256,128]{1,0:T(8,128)(2,1)S(1)}, u32[]{:S(2)}, u32[]{:S(2)}) collective-permute-start(bf16[256,128]{1,0:T(8,128)(2,1)} %param.14), channel_id=1, source_target_pairs={{0,32},{32,64},{64,96},{96,128},{128,160},{160,192},{192,224},{224... | collective-permute-start | bytes 196616 | tf_op jit(solution)/shard_map/ppermute | solution.py:18
  31.5 7.6 %copy-start.3 = (f32[128,2]{0,1:T(2,128)S(1)}, f32[128,2]{0,1:T(2,128)}, u32[]{:S(2)}) copy-start(f32[128,2]{0,1:T(2,128)} %param.13) | copy-start | bytes 3076
  32.9 13.0 %copy-start.5 = (bf16[256,576]{0,1:T(8,128)(2,1)S(1)}, bf16[256,576]{0,1:T(8,128)(2,1)}, u32[]{:S(2)}) copy-start(bf16[256,576]{0,1:T(8,128)(2,1)} %param.10) | copy-start | bytes 884740
  32.9 13.0 %collective-permute-start.5 = (bf16[256,576]{0,1:T(8,128)(2,1)}, bf16[256,576]{0,1:T(8,128)(2,1)S(1)}, u32[]{:S(2)}, u32[]{:S(2)}) collective-permute-start(bf16[256,576]{0,1:T(8,128)(2,1)} %param.10), channel_id=1, source_target_pairs={{0,32},{32,64},{64,96},{96,128},{128,160},{160,192},{192,224},{224... | collective-permute-start | bytes 884744 | tf_op jit(solution)/shard_map/ppermute | solution.py:18
  46.0 1.0 copy-start.1
  47.3 331.6 %copy-start.2 = (s32[128]{0:T(128)S(1)}, s32[128]{0:T(128)}, u32[]{:S(2)}) copy-start(s32[128]{0:T(128)} %param.16) | copy-start | bytes 1540
  47.3 333.3 %copy-start.4 = (f32[128]{0:T(128)S(1)}, f32[128]{0:T(128)}, u32[]{:S(2)}) copy-start(f32[128]{0:T(128)} %param.15) | copy-start | bytes 1540
  48.6 647.9 %all-reduce.5.cloned.1.call-start = ((), (), s32[]{:S(2)}) async-start(), calls=%async_computation | async-start | bytes 262144 | tf_op jit(solution)/shard_map/psum | solution.py:100
  382.5 11.9 %copy-start.6 = (bf16[256,128]{1,0:T(8,128)(2,1)S(1)}, bf16[256,128]{1,0:T(8,128)(2,1)}, u32[]{:S(2)}) copy-start(bf16[256,128]{1,0:T(8,128)(2,1)} %param.14) | copy-start | bytes 196612
  386.5 9.4 %collective-permute-start.6 = (f32[256,128]{1,0:T(8,128)S(1)}, f32[256,128]{1,0:T(8,128)S(1)}, u32[]{:S(2)}, u32[]{:S(2)}) collective-permute-start(f32[256,128]{1,0:T(8,128)S(1)} %get-tuple-element.11), channel_id=1, source_target_pairs={{32,0},{64,32},{96,64},{128,96},{160,128},{192,160},{224,192},{256... | collective-permute-start | bytes 393224 | tf_op jit(solution)/shard_map/ppermute | solution.py:18
  388.4 14.2 %collective-permute-start.7 = (f32[256,128]{1,0:T(8,128)S(1)}, f32[256,128]{1,0:T(8,128)S(1)}, u32[]{:S(2)}, u32[]{:S(2)}) collective-permute-start(f32[256,128]{1,0:T(8,128)S(1)} %get-tuple-element.13), channel_id=1, source_target_pairs={{64,0},{96,32},{128,64},{160,96},{192,128},{224,160},{256,192},{28... | collective-permute-start | bytes 393224 | tf_op jit(solution)/shard_map/ppermute | solution.py:18
  393.1 11.2 %collective-permute-start.8 = (f32[256,128]{1,0:T(8,128)S(1)}, f32[256,128]{1,0:T(8,128)S(1)}, u32[]{:S(2)}, u32[]{:S(2)}) collective-permute-start(f32[256,128]{1,0:T(8,128)S(1)} %get-tuple-element.12), channel_id=1, source_target_pairs={{96,0},{128,32},{160,64},{192,96},{224,128},{256,160},{288,192},{3... | collective-permute-start | bytes 393224 | tf_op jit(solution)/shard_map/ppermute | solution.py:18
Sparse Core Ops, SparseCore 0:
  48.7 330.1 all-reduce.6
  405.1 291.3 all-reduce.4
where the time goes:
time: 705 us
  waiting for transfers between devices  635 us (90%)
  starting transfers between devices  34.9 us (5%)
  between operations  14.3 us (2%)
  other arithmetic  12.1 us (2%)
    psum x1, waiting for transfers between devices, shards(): mass, index_score = lax.psum((mass_part, index_part), 'head')  330 us
    psum x1, waiting for transfers between devices, shards(): grad_keys = lax.psum(grad_total, 'head')  291 us
    ppermute x9, starting transfers between devices, passed_along(): return lax.ppermute(block, axis, route)  34.8 us
    ppermute x9, waiting for transfers between devices, passed_along(): return lax.ppermute(block, axis, route)  14.4 us
  transfers between devices with their start and end apart: 11, of which 5 were waited for; matrix products, arithmetic and copies ran while one was open for 1% of the time, Pallas kernels for 0%

commit v1 on v0

v1 whole, which is shorter than its diff:
```python
import functools

import jax
import jax.numpy as jnp
from jax import lax
from jax.experimental import pallas as pl
from jax.experimental.pallas import tpu as pltpu
from jax.sharding import PartitionSpec as P

MESH = pl.DeviceIdType.MESH
STEPS = 4
IDIM = 128
WIDTH = 576
PAD = 64
WIDE = WIDTH + PAD
NEGATIVE = -1e30
ABSENT = 1e9
SCORE_SCALE = 192.0 ** (-0.5)
FACTOR = IDIM ** (-0.5)
F32 = jnp.float32
BF16 = jnp.bfloat16


def dot(a, b, dims):
    return lax.dot_general(a, b, (dims, ((), ())), preferred_element_type=F32)


def swap(x):
    return pltpu.roll(x, 4, 0)


def split_pair(a, b, low):
    return jnp.where(low, a, swap(b)), jnp.where(low, swap(a), b)


def high_part(x):
    return x.astype(BF16).astype(F32)


def kernel(
    ns,
    nh,
    main_query,
    latent,
    outside,
    index_query,
    index_weights,
    index_keys,
    index_outside,
    query_pos,
    key_pos,
    grad_query,
    grad_weight,
    grad_keys,
    rows,
    cols,
    place,
    queries,
    lat,
    keys,
    wide_query,
    scores,
    ask_out,
    ask_in,
    mass_out,
    mass_in,
    near_query,
    near_weight,
    act,
    upper,
    lower,
    rest_weight,
    terms_out,
    terms_in,
    back_out,
    back_in,
    part_out,
    part_in,
    final,
    wide_grad,
    weight_grad,
    local_sem,
    lat_send,
    lat_recv,
    key_send,
    key_recv,
    ask_sem,
    mass_sem,
    terms_sem,
    back_sem,
    part_send,
    part_recv,
    final_sem,
):
    q_rows = index_query.shape[0]
    kb = key_pos.shape[1]
    window = STEPS * kb
    half = window // 2
    chunks = q_rows // 8
    blocks = kb // 128
    tiles = 16 * blocks
    per = tiles // nh
    head = lax.axis_index("head")
    seq = lax.axis_index("seq")

    local = []
    for parity in range(2):
        for i in range(2):
            start = (2 * i + parity) * WIDTH - parity * PAD
            local.append(
                pltpu.make_async_copy(
                    main_query.at[:, pl.ds(start, WIDE)],
                    queries.at[parity, pl.ds(i * q_rows, q_rows), :],
                    local_sem.at[2 * parity + i],
                )
            )
    local.append(
        pltpu.make_async_copy(latent, lat.at[STEPS - 1, pl.ds(PAD, WIDTH), :], local_sem.at[4])
    )
    local.append(pltpu.make_async_copy(index_keys, keys.at[STEPS - 1], local_sem.at[5]))
    for copy in local:
        copy.start()

    barrier = pltpu.get_barrier_semaphore()

    def greet(r, carry):
        pl.semaphore_signal(
            barrier, inc=1, device_id={"head": lax.rem(head + r, nh)}, device_id_type=MESH
        )
        return carry

    for distance in range(1, STEPS):
        for other in (seq + distance, seq + ns - distance):
            pl.semaphore_signal(
                barrier, inc=1, device_id={"seq": lax.rem(other, ns)}, device_id_type=MESH
            )
    lax.fori_loop(1, nh, greet, 0)

    low = lax.broadcasted_iota(jnp.int32, (8, 128), 0) < 4
    lane = lax.broadcasted_iota(jnp.int32, (8, 128), 1)
    rows[...] = jnp.zeros_like(rows)
    rows[0:4, :] = outside[...]
    rows[4:6, :] = index_weights[...]
    rows[6:7, :] = query_pos[...].astype(F32)
    rows[7:8, :] = index_outside[...]
    cols[...] = rows[...].T
    for k in range(STEPS):
        here = jnp.where(seq >= STEPS - 1 - k, 0.0, ABSENT)
        own = key_pos[...].astype(F32) if k == STEPS - 1 else jnp.zeros((1, kb), F32)
        place[:, k * kb : (k + 1) * kb] = own + here
        lat[k, 0:PAD, :] = jnp.zeros((PAD, kb), BF16)
        lat[k, PAD + WIDTH : PAD + WIDTH + PAD, :] = jnp.zeros((PAD, kb), BF16)
    wide_query[...] = index_query[...].astype(F32)

    def ask(c, carry):
        at = pl.ds(pl.multiple_of(8 * c, 8), 8)
        values = wide_query[at, :]
        column = cols[at, :]
        first = jnp.broadcast_to(column[:, 4:5], (8, 128))
        second = jnp.broadcast_to(column[:, 5:6], (8, 128))
        pair = split_pair(values[:, :IDIM], values[:, IDIM:], low)
        weights = split_pair(first, second, low)
        for i in range(2):
            weight = weights[i]
            top = high_part(weight)
            mid = high_part(weight - top)
            end = weight - top - mid
            packed = jnp.where(lane == 0, top, jnp.where(lane == 1, mid, end))
            ask_out[2 * c + i] = jnp.concatenate([pair[i], packed], 0).astype(BF16)
        return carry

    lax.fori_loop(0, chunks, ask, 0)

    pl.semaphore_wait(barrier, nh - 1 + 2 * (STEPS - 1))

    lat_copies = []
    key_copies = []
    for distance in range(1, STEPS):
        target = {"seq": lax.rem(seq + distance, ns)}
        slot = STEPS - 1 - distance
        copy = pltpu.make_async_remote_copy(
            src_ref=latent,
            dst_ref=lat.at[slot, pl.ds(PAD, WIDTH), :],
            send_sem=lat_send.at[slot],
            recv_sem=lat_recv.at[slot],
            device_id=target,
            device_id_type=MESH,
        )
        copy.start()
        lat_copies.append(copy)
    for distance in range(1, STEPS):
        target = {"seq": lax.rem(seq + distance, ns)}
        slot = STEPS - 1 - distance
        copy = pltpu.make_async_remote_copy(
            src_ref=index_keys,
            dst_ref=keys.at[slot],
            send_sem=key_send.at[slot],
            recv_sem=key_recv.at[slot],
            device_id=target,
            device_id_type=MESH,
        )
        copy.start()
        key_copies.append(copy)

    def exchange(source, target, sems, peer, slot):
        return pltpu.make_async_remote_copy(
            src_ref=source,
            dst_ref=target,
            send_sem=sems.at[0],
            recv_sem=sems.at[1],
            device_id={"head": peer},
            device_id_type=MESH,
        )

    def send_ask(r, carry):
        peer = lax.rem(head + r, nh)
        exchange(ask_out.at[peer], ask_in.at[nh - 1 - r], ask_sem, peer, 0).start()
        return carry

    lax.fori_loop(1, nh, send_ask, 0)
    ask_in[nh - 1] = ask_out[head]

    def all_of(source, target, sems):
        return exchange(
            source.at[pl.ds(0, nh - 1)], target.at[pl.ds(0, nh - 1)], sems, lax.rem(head + 1, nh), 0
        )

    for copy in local:
        copy.wait()
    for k in range(STEPS - 1, -1, -1):
        if k < STEPS - 1:
            lat_copies[STEPS - 2 - k].wait_recv()
        for parity in range(2):
            table = lat[k, PAD * (1 - parity) : PAD * (1 - parity) + WIDE, :]
            scores[parity, :, k * kb : (k + 1) * kb] = (
                dot(queries[parity], table, ((1,), (0,))) * SCORE_SCALE
            )

    def soften(step, carry):
        c = lax.rem(step + head // 2 + 1, chunks)
        at = pl.ds(pl.multiple_of(8 * c, 8), 8)
        column = cols[at, :]
        visible = place[...] <= column[:, 6:7]
        mass = jnp.zeros((8, window), F32)
        for parity in range(2):
            for i in range(2):
                h = 2 * i + parity
                from_row = pl.multiple_of(i * q_rows + 8 * c, 8)
                x = jnp.where(visible, scores[parity, pl.ds(from_row, 8), :], NEGATIVE)
                out = column[:, h : h + 1]
                top = jnp.maximum(jnp.max(x, axis=1, keepdims=True), out)
                e = jnp.exp(x - top)
                total = jnp.sum(e, axis=1, keepdims=True) + jnp.exp(out - top)
                mass = mass + e * (1.0 / total)
        halves = split_pair(
            mass[:, :half], mass[:, half:], lax.broadcasted_iota(jnp.int32, (8, half), 0) < 4
        )
        for i in range(2):
            peer = 2 * c + i
            mass_out[peer] = halves[i]

            @pl.when(peer != head)
            def _():
                r = lax.rem(peer + nh - head, nh)
                exchange(mass_out.at[peer], mass_in.at[nh - 1 - r], mass_sem, peer, 0).start()

        return carry

    lax.fori_loop(0, chunks, soften, 0)
    mass_in[nh - 1] = mass_out[head]

    all_of(ask_out, ask_in, ask_sem).wait_recv()

    def unpack(g, carry):
        at = pl.ds(pl.multiple_of(8 * g, 8), 8)
        both = ask_in[g].astype(F32)
        near_query[at, :] = both[0:8, :]
        packed = both[8:16, :]
        weight = packed[:, 0:1] + (packed[:, 1:2] + packed[:, 2:3])
        near_weight[at, :] = jnp.broadcast_to(weight, (8, 128))
        return carry

    lax.fori_loop(0, nh, unpack, 0)
    asked = near_query[...].astype(BF16)
    for k in range(STEPS - 1, -1, -1):
        if k < STEPS - 1:
            key_copies[STEPS - 2 - k].wait_recv()
        act[:, k * kb : (k + 1) * kb] = dot(asked, keys[k], ((1,), (1,))) * FACTOR

    def add_score(g, total):
        at = pl.ds(pl.multiple_of(8 * g, 8), 8)
        return total + near_weight[at, 0:1] * jnp.maximum(act[at, :], 0.0)

    score = lax.fori_loop(0, nh, add_score, jnp.zeros((8, window), F32))
    score = score + swap(score)
    odd = lax.rem(head, 2)
    column = cols[pl.ds(pl.multiple_of(8 * (head // 2), 8), 8), :]
    pick = (lax.broadcasted_iota(jnp.int32, (8, 128), 0) // 4) == odd
    column = jnp.where(pick, column, swap(column))
    visible = place[...] <= column[:, 6:7]
    masked = jnp.where(visible, score, NEGATIVE)
    limit = column[:, 7:8]
    top = jnp.maximum(jnp.max(masked, axis=1, keepdims=True), limit)
    e = jnp.exp(masked - top)
    total = jnp.sum(e, axis=1, keepdims=True) + jnp.exp(limit - top)
    predicted = e * (1.0 / total)
    weighted = near_weight[...] * near_query[...]
    turned = weighted.T
    turned_high = turned.astype(BF16)
    turned_low = (turned - turned_high.astype(F32)).astype(BF16)

    all_of(mass_out, mass_in, mass_sem).wait_recv()
    mass = mass_in[0]
    for g in range(1, nh):
        mass = mass + mass_in[g]
    low_half = lax.broadcasted_iota(jnp.int32, (8, half), 0) < 4
    turned_mass = swap(mass)
    mass = jnp.concatenate(
        [jnp.where(low_half, mass, turned_mass), jnp.where(low_half, turned_mass, mass)], 1
    )
    target = mass * (1.0 / jnp.sum(mass, axis=1, keepdims=True))
    dscore = (predicted - target) * float(window)
    d_high = high_part(dscore)
    d_low = dscore - d_high

    def gate(g, carry):
        at = pl.ds(pl.multiple_of(16 * g, 16), 16)
        a = act[at, :]
        on = a > 0.0
        upper[at, :] = jnp.where(on, jnp.concatenate([d_high, d_high], 0), 0.0).astype(BF16)
        lower[at, :] = jnp.where(on, jnp.concatenate([d_low, d_low], 0), 0.0).astype(BF16)
        share = jnp.sum(
            jnp.concatenate([dscore, dscore], 0) * jnp.maximum(a, 0.0), axis=1, keepdims=True
        )
        rest_weight[at, :] = jnp.broadcast_to(share, (16, 128))
        return carry

    lax.fori_loop(0, nh // 2, gate, 0)

    for k in range(STEPS):
        at = slice(k * kb, (k + 1) * kb)
        high_block = upper[:, at]
        terms = dot(turned_high, high_block, ((1,), (0,)))
        terms = terms + dot(turned_low, high_block, ((1,), (0,)))
        terms = terms + dot(turned_high, lower[:, at], ((1,), (0,)))
        terms = terms * FACTOR
        for tile in range(tiles):
            d, b = tile // blocks, tile % blocks
            terms_out[tile // per, k, tile % per] = terms[
                8 * d : 8 * d + 8, 128 * b : 128 * b + 128
            ]

    def send_terms(r, carry):
        peer = lax.rem(head + r, nh)
        exchange(terms_out.at[peer], terms_in.at[nh - 1 - r], terms_sem, peer, 0).start()
        return carry

    lax.fori_loop(1, nh, send_terms, 0)
    terms_in[nh - 1] = terms_out[head]

    all_keys = keys[...].reshape(window, IDIM)
    near_grad = dot(upper[...], all_keys, ((1,), (0,))) + dot(lower[...], all_keys, ((1,), (0,)))
    wide_grad[...] = near_grad * FACTOR * near_weight[...]

    def pack_back(g, carry):
        at = pl.ds(pl.multiple_of(8 * g, 8), 8)
        share = rest_weight[at, :]
        top = high_part(share)
        mid = high_part(share - top)
        packed = jnp.where(lane == 0, top, jnp.where(lane == 1, mid, share - top - mid))
        back_out[g] = jnp.concatenate([wide_grad[at, :], packed], 0).astype(BF16)
        return carry

    lax.fori_loop(0, nh, pack_back, 0)

    def send_back(r, carry):
        peer = lax.rem(head + r, nh)
        exchange(back_out.at[r - 1], back_in.at[head], back_sem, peer, 0).start()
        return carry

    lax.fori_loop(1, nh, send_back, 0)
    back_in[head] = back_out[nh - 1]

    all_of(terms_out, terms_in, terms_sem).wait_recv()
    summed = terms_in[0]
    for g in range(1, nh):
        summed = summed + terms_in[g]
    part_out[...] = summed
    part_copies = []
    for k in range(STEPS - 1):
        distance = STEPS - 1 - k
        copy = pltpu.make_async_remote_copy(
            src_ref=part_out.at[k],
            dst_ref=part_in.at[k],
            send_sem=part_send.at[k],
            recv_sem=part_recv.at[k],
            device_id={"seq": lax.rem(seq + ns - distance, ns)},
            device_id_type=MESH,
        )
        copy.start()
        part_copies.append(copy)
    mine = part_out[STEPS - 1]
    for copy in part_copies:
        copy.wait_recv()
    for k in range(STEPS - 1):
        mine = mine + part_in[k]
    final[head] = mine

    def send_final(r, carry):
        peer = lax.rem(head + r, nh)
        exchange(final.at[head], final.at[head], final_sem, peer, 0).start()
        return carry

    lax.fori_loop(1, nh, send_final, 0)

    all_of(back_out, back_in, back_sem).wait_recv()

    def unpack_back(c, carry):
        at = pl.ds(pl.multiple_of(8 * c, 8), 8)
        one = back_in[2 * c].astype(F32)
        two = back_in[2 * c + 1].astype(F32)
        first, second = split_pair(one[0:8, :], two[0:8, :], low)
        wide_query[at, 0:IDIM] = first
        wide_query[at, IDIM : 2 * IDIM] = second
        shares = []
        for packed in (one[8:16, :], two[8:16, :]):
            share = packed[:, 0:1] + (packed[:, 1:2] + packed[:, 2:3])
            shares.append(jnp.broadcast_to(share, (8, 128)))
        first, second = split_pair(shares[0], shares[1], low)
        weight_grad[at, :] = jnp.where(lane == 0, first, second)
        return carry

    lax.fori_loop(0, chunks, unpack_back, 0)
    grad_query[...] = wide_query[...].astype(BF16)
    grad_weight[...] = weight_grad[...].T[0:2, :]

    all_of(final, final, final_sem).wait_recv()
    for b in range(blocks):
        columns = [final[(d * blocks + b) // per, (d * blocks + b) % per] for d in range(16)]
        grad_keys[128 * b : 128 * b + 128, :] = jnp.concatenate(columns, 0).T

    for copy in lat_copies + key_copies + part_copies:
        copy.wait_send()
    all_of(ask_out, ask_in, ask_sem).wait_send()
    all_of(mass_out, mass_in, mass_sem).wait_send()
    all_of(terms_out, terms_in, terms_sem).wait_send()
    all_of(back_out, back_in, back_sem).wait_send()
    all_of(final, final, final_sem).wait_send()


def solution(mesh):
    ns, nh = mesh.shape["seq"], mesh.shape["head"]

    def shards(
        main_query,
        latent,
        main_outside,
        index_query,
        index_weights,
        index_keys,
        index_outside,
        query_pos,
        key_pos,
    ):
        q = main_query.shape[0]
        kb = latent.shape[0]
        window = STEPS * kb
        per = 16 * (kb // 128) // nh
        vmem = pl.BlockSpec(memory_space=pltpu.VMEM)
        whole = pl.BlockSpec(memory_space=pl.ANY)
        dma = pltpu.SemaphoreType.DMA
        grad_query, grad_weight, grad_keys = pl.pallas_call(
            functools.partial(kernel, ns, nh),
            out_shape=(
                jax.ShapeDtypeStruct((q, 2 * IDIM), BF16),
                jax.ShapeDtypeStruct((2, q), F32),
                jax.ShapeDtypeStruct((kb, IDIM), F32),
            ),
            in_specs=[whole, whole, vmem, vmem, vmem, whole, vmem, vmem, vmem],
            out_specs=(vmem, vmem, vmem),
            scratch_shapes=[
                pltpu.VMEM((128, q), F32),
                pltpu.VMEM((q, 128), F32),
                pltpu.VMEM((1, window), F32),
                pltpu.VMEM((2, 2 * q, WIDE), BF16),
                pltpu.VMEM((STEPS, WIDE + PAD, kb), BF16),
                pltpu.VMEM((STEPS, kb, IDIM), BF16),
                pltpu.VMEM((q, 2 * IDIM), F32),
                pltpu.VMEM((2, 2 * q, window), F32),
                pltpu.VMEM((nh, 16, 128), BF16),
                pltpu.VMEM((nh, 16, 128), BF16),
                pltpu.VMEM((nh, 8, window // 2), F32),
                pltpu.VMEM((nh, 8, window // 2), F32),
                pltpu.VMEM((8 * nh, 128), F32),
                pltpu.VMEM((8 * nh, 128), F32),
                pltpu.VMEM((8 * nh, window), F32),
                pltpu.VMEM((8 * nh, window), BF16),
                pltpu.VMEM((8 * nh, window), BF16),
                pltpu.VMEM((8 * nh, 128), F32),
                pltpu.VMEM((nh, STEPS, per, 8, 128), F32),
                pltpu.VMEM((nh, STEPS, per, 8, 128), F32),
                pltpu.VMEM((nh, 16, 128), BF16),
                pltpu.VMEM((nh, 16, 128), BF16),
                pltpu.VMEM((STEPS, per, 8, 128), F32),
                pltpu.VMEM((STEPS - 1, per, 8, 128), F32),
                pltpu.VMEM((nh, per, 8, 128), F32),
                pltpu.VMEM((8 * nh, 128), F32),
                pltpu.VMEM((q, 128), F32),
                dma((6,)),
                dma((STEPS - 1,)),
                dma((STEPS - 1,)),
                dma((STEPS - 1,)),
                dma((STEPS - 1,)),
                dma((2,)),
                dma((2,)),
                dma((2,)),
                dma((2,)),
                dma((STEPS - 1,)),
                dma((STEPS - 1,)),
                dma((2,)),
            ],
            compiler_params=pltpu.CompilerParams(
                collective_id=0, has_side_effects=True, vmem_limit_bytes=48 << 20
            ),
        )(
            main_query,
            latent.T,
            main_outside.T,
            index_query,
            index_weights.T,
            index_keys,
            index_outside.reshape(1, q),
            query_pos.reshape(1, q),
            key_pos.reshape(1, kb),
        )
        return grad_query, grad_weight.T, grad_keys

    in_specs = (
        P("seq", "head"),
        P("seq", None),
        P("seq", "head"),
        P("seq", "head"),
        P("seq", "head"),
        P("seq", None),
        P("seq"),
        P("seq"),
        P("seq"),
    )
    out_specs = (P("seq", "head"), P("seq", "head"), P("seq", None))
    return jax.shard_map(shards, mesh=mesh, in_specs=in_specs, out_specs=out_specs, check_vma=False)
```

time: 705 us -> 109 us (0.15)
  the two profiles are of different devices: /device:TPU:14 before, /device:TPU:1 now
where the time goes in v1:
time: 109 us; the launch traced here: 107 us
  Pallas kernels  100 us (92%)
  local copies, waits for them, and re-layouts  6.24 us (6%)
    pallas_call x1, Pallas kernels, shards(): pl.pallas_call(functools.partial(kernel, ns, nh), out_shape=(jax.ShapeDty...  100 us
    unnamed x21, local copies, waits for them, and re-layouts  6.24 us

profile of v1, /device:TPU:1, one launch (start us, length us, event | category | flops | bytes accessed | tf_op | source)
XLA Modules:
  0.0 107.2 jit_solution(6619257450172647463)
XLA Ops:
  0.6 0.0 copy-start.6
  0.6 0.0 copy-start.8
  0.7 0.0 copy-start.4
  0.7 0.0 copy-start.5
  0.7 0.0 copy-start.7
  0.7 0.6 copy-done.6
  1.3 0.0 copy-done.8
  1.3 0.0 copy-done.4
  1.3 0.0 copy-done.5
  1.4 0.0 copy-done.7
  1.4 0.0 copy-start
  1.4 1.1 copy-done
  2.4 0.0 copy-start.1
  2.4 1.0 copy-done.1
  3.4 0.0 copy-start.2
  3.4 0.8 copy-done.2
  4.2 0.0 copy-start.3
  4.2 0.8 copy-done.3
  5.1 100.3 %shard_map.112 = (bf16[128,256]{1,0:T(8,128)(2,1)S(1)}, f32[2,128]{1,0:T(2,128)S(1)}, f32[256,128]{1,0:T(8,128)S(1)}) custom-call(bf16[128,2304]{1,0:T(8,128)(2,1)S(1)} %copy-done, bf16[576,256]{1,0:T(8,128)(2,1)S(1)} %bitcast.7, f32[4,128]{1,0:T(4,128)S(1)} %bitcast.8, bf16[128,256]{1,0:T(8,128)(2,1)S(1)} %copy-done.2, f32[2,128]{1,0:T(2,128)S(1)} %bitcast.9, ...), custom_call_target="tpu_custom_call" | custom-call | tf_op jit(solution)/shard_map/pallas_call | solution.py:472
  105.4 0.6 copy.15
  106.0 0.6 copy.16
  106.6 0.7 copy.17
Async XLA Ops:
  0.6 0.7 copy-start.6
  0.6 0.7 copy-start.8
  0.7 0.7 copy-start.4
  0.7 0.7 copy-start.5
  0.7 0.7 copy-start.7
  1.4 1.1 copy-start
  2.4 1.0 copy-start.1
  3.4 0.8 copy-start.2
  4.2 0.8 copy-start.3

commit v2 on v1

--- a/solution.py
+++ b/solution.py
@@ -13,6 +13,9 @@
 WIDTH = 576
 PAD = 64
 WIDE = WIDTH + PAD
+X_RUN = 4
+X_ROWS = 320
+Z_ROWS = WIDTH - X_ROWS
 NEGATIVE = -1e30
 ABSENT = 1e9
 SCORE_SCALE = 192.0 ** (-0.5)
@@ -58,6 +61,7 @@
     queries,
     lat,
     keys,
+    narrow_query,
     wide_query,
     scores,
     ask_out,
@@ -80,10 +84,14 @@
     wide_grad,
     weight_grad,
     local_sem,
-    lat_send,
-    lat_recv,
-    key_send,
-    key_recv,
+    cross_send,
+    cross_recv,
+    direct_send,
+    direct_recv,
+    gather_send,
+    gather_recv,
+    forward_send,
+    forward_recv,
     ask_sem,
     mass_sem,
     terms_sem,
@@ -118,6 +126,7 @@
         pltpu.make_async_copy(latent, lat.at[STEPS - 1, pl.ds(PAD, WIDTH), :], local_sem.at[4])
     )
     local.append(pltpu.make_async_copy(index_keys, keys.at[STEPS - 1], local_sem.at[5]))
+    local.append(pltpu.make_async_copy(index_query, narrow_query, local_sem.at[6]))
     for copy in local:
         copy.start()
 
@@ -150,7 +159,8 @@
         place[:, k * kb : (k + 1) * kb] = own + here
         lat[k, 0:PAD, :] = jnp.zeros((PAD, kb), BF16)
         lat[k, PAD + WIDTH : PAD + WIDTH + PAD, :] = jnp.zeros((PAD, kb), BF16)
-    wide_query[...] = index_query[...].astype(F32)
+    local[6].wait()
+    wide_query[...] = narrow_query[...].astype(F32)
 
     def ask(c, carry):
         at = pl.ds(pl.multiple_of(8 * c, 8), 8)
@@ -173,34 +183,57 @@
 
     pl.semaphore_wait(barrier, nh - 1 + 2 * (STEPS - 1))
 
-    lat_copies = []
-    key_copies = []
-    for distance in range(1, STEPS):
-        target = {"seq": lax.rem(seq + distance, ns)}
-        slot = STEPS - 1 - distance
-        copy = pltpu.make_async_remote_copy(
-            src_ref=latent,
-            dst_ref=lat.at[slot, pl.ds(PAD, WIDTH), :],
-            send_sem=lat_send.at[slot],
-            recv_sem=lat_recv.at[slot],
-            device_id=target,
+    core = lax.rem(seq, 2)
+    early, late = 2 * core, 2 - 2 * core
+    ring, run = head // X_RUN, lax.rem(head, X_RUN)
+    rings = nh // X_RUN
+    run_rows, ring_rows, key_rows = X_ROWS // X_RUN, Z_ROWS // rings, kb // rings
+    run_at = pl.multiple_of(run_rows * run, 16)
+    ring_at = pl.multiple_of(X_ROWS + ring_rows * ring, 16)
+    key_at = pl.multiple_of(key_rows * ring, 16)
+
+    def lat_rows(slot, start, size):
+        return lat.at[slot, pl.ds(pl.multiple_of(PAD + start, 16), size), :]
+
+    def key_part(slot, start, size):
+        return keys.at[slot, pl.ds(start, size), :]
+
+    def to_seq(source, target, send, recv, i, other):
+        return pltpu.make_async_remote_copy(
+            src_ref=source,
+            dst_ref=target,
+            send_sem=send.at[i],
+            recv_sem=recv.at[i],
+            device_id={"seq": other},
             device_id_type=MESH,
         )
+
+    two = lax.rem(seq + 2, ns)
+    sibling = seq + 1 - 2 * core
+    crossing = [
+        to_seq(
+            index_keys.at[pl.ds(key_at, key_rows), :],
+            key_part(1, key_at, key_rows),
+            cross_send, cross_recv, 0, two,
+        ),
+        to_seq(
+            latent.at[pl.ds(ring_at, ring_rows), :],
+            lat_rows(1, ring_at, ring_rows),
+            cross_send, cross_recv, 1, two,
+        ),
+        to_seq(
+            latent.at[pl.ds(run_at, run_rows), :],
+            lat_rows(1, run_at, run_rows),
+            cross_send, cross_recv, 2, two,
+        ),
+    ]
+    onward = lax.rem(seq + 1 + 2 * core, ns)
+    direct = [
+        to_seq(index_keys, keys.at[late], direct_send, direct_recv, 0, onward),
+        to_seq(latent, lat_rows(late, 0, WIDTH), direct_send, direct_recv, 1, onward),
+    ]
+    for copy in crossing + direct:
         copy.start()
-        lat_copies.append(copy)
-    for distance in range(1, STEPS):
-        target = {"seq": lax.rem(seq + distance, ns)}
-        slot = STEPS - 1 - distance
-        copy = pltpu.make_async_remote_copy(
-            src_ref=index_keys,
-            dst_ref=keys.at[slot],
-            send_sem=key_send.at[slot],
-            recv_sem=key_recv.at[slot],
-            device_id=target,
-            device_id_type=MESH,
-        )
-        copy.start()
-        key_copies.append(copy)
 
     def exchange(source, target, sems, peer, slot):
         return pltpu.make_async_remote_copy(
@@ -225,16 +258,90 @@
             source.at[pl.ds(0, nh - 1)], target.at[pl.ds(0, nh - 1)], sems, lax.rem(head + 1, nh), 0
         )
 
-    for copy in local:
-        copy.wait()
-    for k in range(STEPS - 1, -1, -1):
-        if k < STEPS - 1:
-            lat_copies[STEPS - 2 - k].wait_recv()
+    def score_block(k):
+        at = pl.ds(pl.multiple_of(k * kb, 128), kb)
         for parity in range(2):
             table = lat[k, PAD * (1 - parity) : PAD * (1 - parity) + WIDE, :]
-            scores[parity, :, k * kb : (k + 1) * kb] = (
-                dot(queries[parity], table, ((1,), (0,))) * SCORE_SCALE
-            )
+            scores[parity, :, at] = dot(queries[parity], table, ((1,), (0,))) * SCORE_SCALE
+
+    def act_block(k, asked):
+        at = pl.ds(pl.multiple_of(k * kb, 128), kb)
+        act[:, at] = dot(asked, keys[k], ((1,), (1,))) * FACTOR
+
+    def to_head(part, i, peer):
+        return pltpu.make_async_remote_copy(
+            src_ref=part,
+            dst_ref=part,
+            send_sem=gather_send.at[i],
+            recv_sem=gather_recv.at[i],
+            device_id={"head": peer},
+            device_id_type=MESH,
+        )
+
+    for copy in local[:6]:
+        copy.wait()
+    score_block(STEPS - 1)
+    for copy in crossing:
+        copy.wait_recv()
+
+    def push_ring(r, carry):
+        peer = lax.rem(head + r * X_RUN, nh)
+        to_head(key_part(1, key_at, key_rows), 0, peer).start()
+        to_head(lat_rows(1, ring_at, ring_rows), 1, peer).start()
+        return carry
+
+    def push_run(r, carry):
+        peer = ring * X_RUN + lax.rem(run + r, X_RUN)
+        to_head(lat_rows(1, run_at, run_rows), 2, peer).start()
+        return carry
+
+    lax.fori_loop(1, rings, push_ring, 0)
+    lax.fori_loop(1, X_RUN, push_run, 0)
+    gathered = [
+        to_head(key_part(1, 0, key_rows * (rings - 1)), 0, head),
+        to_head(lat_rows(1, 0, ring_rows * (rings - 1)), 1, head),
+        to_head(lat_rows(1, 0, run_rows * (X_RUN - 1)), 2, head),
+    ]
+    forward = [
+        to_seq(keys.at[1], keys.at[early], forward_send, forward_recv, 0, sibling),
+        to_seq(
+            lat_rows(1, X_ROWS, Z_ROWS),
+            lat_rows(early, X_ROWS, Z_ROWS),
+            forward_send, forward_recv, 1, sibling,
+        ),
+        to_seq(
+            lat_rows(1, 0, X_ROWS),
+            lat_rows(early, 0, X_ROWS),
+            forward_send, forward_recv, 2, sibling,
+        ),
+    ]
+    for copy in direct:
+        copy.wait_recv()
+    score_block(early)
+    for i in range(3):
+        gathered[i].wait_recv()
+        forward[i].start()
+    score_block(1)
+
+    all_of(ask_out, ask_in, ask_sem).wait_recv()
+
+    def unpack(g, carry):
+        at = pl.ds(pl.multiple_of(8 * g, 8), 8)
+        both = ask_in[g].astype(F32)
+        near_query[at, :] = both[0:8, :]
+        packed = both[8:16, :]
+        weight = packed[:, 0:1] + (packed[:, 1:2] + packed[:, 2:3])
+        near_weight[at, :] = jnp.broadcast_to(weight, (8, 128))
+        return carry
+
+    lax.fori_loop(0, nh, unpack, 0)
+    asked = near_query[...].astype(BF16)
+    act_block(STEPS - 1, asked)
+    act_block(early, asked)
+    act_block(1, asked)
+    forward[1].wait_recv()
+    forward[2].wait_recv()
+    score_block(late)
 
     def soften(step, carry):
         c = lax.rem(step + head // 2 + 1, chunks)
@@ -257,7 +364,9 @@
         )
         for i in range(2):
             peer = 2 * c + i
-            mass_out[peer] = halves[i]
+            mass_out[peer] = jnp.concatenate(
+                [halves[i][:, : half // 2], halves[i][:, half // 2 :]], 0
+            ).astype(BF16)
 
             @pl.when(peer != head)
             def _():
@@ -269,23 +378,8 @@
     lax.fori_loop(0, chunks, soften, 0)
     mass_in[nh - 1] = mass_out[head]
 
-    all_of(ask_out, ask_in, ask_sem).wait_recv()
-
-    def unpack(g, carry):
-        at = pl.ds(pl.multiple_of(8 * g, 8), 8)
-        both = ask_in[g].astype(F32)
-        near_query[at, :] = both[0:8, :]
-        packed = both[8:16, :]
-        weight = packed[:, 0:1] + (packed[:, 1:2] + packed[:, 2:3])
-        near_weight[at, :] = jnp.broadcast_to(weight, (8, 128))
-        return carry
-
-    lax.fori_loop(0, nh, unpack, 0)
-    asked = near_query[...].astype(BF16)
-    for k in range(STEPS - 1, -1, -1):
-        if k < STEPS - 1:
-            key_copies[STEPS - 2 - k].wait_recv()
-        act[:, k * kb : (k + 1) * kb] = dot(asked, keys[k], ((1,), (1,))) * FACTOR
+    forward[0].wait_recv()
+    act_block(late, asked)
 
     def add_score(g, total):
         at = pl.ds(pl.multiple_of(8 * g, 8), 8)
@@ -310,9 +404,10 @@
     turned_low = (turned - turned_high.astype(F32)).astype(BF16)
 
     all_of(mass_out, mass_in, mass_sem).wait_recv()
-    mass = mass_in[0]
+    mass = mass_in[0].astype(F32)
     for g in range(1, nh):
-        mass = mass + mass_in[g]
+        mass = mass + mass_in[g].astype(F32)
+    mass = jnp.concatenate([mass[0:8, :], mass[8:16, :]], 1)
     low_half = lax.broadcasted_iota(jnp.int32, (8, half), 0) < 4
     turned_mass = swap(mass)
     mass = jnp.concatenate(
@@ -439,7 +534,7 @@
         columns = [final[(d * blocks + b) // per, (d * blocks + b) % per] for d in range(16)]
         grad_keys[128 * b : 128 * b + 128, :] = jnp.concatenate(columns, 0).T
 
-    for copy in lat_copies + key_copies + part_copies:
+    for copy in crossing + direct + gathered + forward + part_copies:
         copy.wait_send()
     all_of(ask_out, ask_in, ask_sem).wait_send()
     all_of(mass_out, mass_in, mass_sem).wait_send()
@@ -467,7 +562,7 @@
         window = STEPS * kb
         per = 16 * (kb // 128) // nh
         vmem = pl.BlockSpec(memory_space=pltpu.VMEM)
-        whole = pl.BlockSpec(memory_space=pl.ANY)
+        whole = pl.BlockSpec(memory_space=pltpu.MemorySpace.HBM)
         dma = pltpu.SemaphoreType.DMA
         grad_query, grad_weight, grad_keys = pl.pallas_call(
             functools.partial(kernel, ns, nh),
@@ -476,7 +571,7 @@
                 jax.ShapeDtypeStruct((2, q), F32),
                 jax.ShapeDtypeStruct((kb, IDIM), F32),
             ),
-            in_specs=[whole, whole, vmem, vmem, vmem, whole, vmem, vmem, vmem],
+            in_specs=[whole, whole, vmem, whole, vmem, whole, vmem, vmem, vmem],
             out_specs=(vmem, vmem, vmem),
             scratch_shapes=[
                 pltpu.VMEM((128, q), F32),
@@ -485,12 +580,13 @@
                 pltpu.VMEM((2, 2 * q, WIDE), BF16),
                 pltpu.VMEM((STEPS, WIDE + PAD, kb), BF16),
                 pltpu.VMEM((STEPS, kb, IDIM), BF16),
+                pltpu.VMEM((q, 2 * IDIM), BF16),
                 pltpu.VMEM((q, 2 * IDIM), F32),
                 pltpu.VMEM((2, 2 * q, window), F32),
                 pltpu.VMEM((nh, 16, 128), BF16),
                 pltpu.VMEM((nh, 16, 128), BF16),
-                pltpu.VMEM((nh, 8, window // 2), F32),
-                pltpu.VMEM((nh, 8, window // 2), F32),
+                pltpu.VMEM((nh, 16, window // 4), BF16),
+                pltpu.VMEM((nh, 16, window // 4), BF16),
                 pltpu.VMEM((8 * nh, 128), F32),
                 pltpu.VMEM((8 * nh, 128), F32),
                 pltpu.VMEM((8 * nh, window), F32),
@@ -506,11 +602,15 @@
                 pltpu.VMEM((nh, per, 8, 128), F32),
                 pltpu.VMEM((8 * nh, 128), F32),
                 pltpu.VMEM((q, 128), F32),
-                dma((6,)),
-                dma((STEPS - 1,)),
-                dma((STEPS - 1,)),
-                dma((STEPS - 1,)),
-                dma((STEPS - 1,)),
+                dma((7,)),
+                dma((3,)),
+                dma((3,)),
+                dma((2,)),
+                dma((2,)),
+                dma((3,)),
+                dma((3,)),
+                dma((3,)),
+                dma((3,)),
                 dma((2,)),
                 dma((2,)),
                 dma((2,)),
@@ -523,12 +623,12 @@
                 collective_id=0, has_side_effects=True, vmem_limit_bytes=48 << 20
             ),
         )(
-            main_query,
-            latent.T,
+            pltpu.with_memory_space_constraint(main_query, pltpu.MemorySpace.HBM),
+            pltpu.with_memory_space_constraint(latent.T, pltpu.MemorySpace.HBM),
             main_outside.T,
-            index_query,
+            pltpu.with_memory_space_constraint(index_query, pltpu.MemorySpace.HBM),
             index_weights.T,
-            index_keys,
+            pltpu.with_memory_space_constraint(index_keys, pltpu.MemorySpace.HBM),
             index_outside.reshape(1, q),
             query_pos.reshape(1, q),
             key_pos.reshape(1, kb),

time: 109 us -> 87.7 us (0.80); the launches traced: 107 us -> 87.6 us
  Pallas kernels: 100 us -> 84.3 us
  local copies, waits for them, and re-layouts: 6.24 us -> 2.54 us
    pallas_call x1, Pallas kernels: 100 us -> 84.3 us  [shards(): pl.pallas_call(functools.partial(kernel, ns, nh), out_shape=(jax.ShapeDty...]
    unnamed x21 -> x13, local copies, waits for them, and re-layouts: 6.24 us -> 2.54 us
where the time goes in v2:
time: 87.7 us; the launch traced here: 87.6 us
  Pallas kernels  84.3 us (96%)
  local copies, waits for them, and re-layouts  2.54 us (3%)
    pallas_call x1, Pallas kernels, shards(): pl.pallas_call(functools.partial(kernel, ns, nh), out_shape=(jax.ShapeDty...  84.3 us
    unnamed x13, local copies, waits for them, and re-layouts  2.54 us

profile of v2, /device:TPU:1, one launch (start us, length us, event | category | flops | bytes accessed | tf_op | source)
XLA Modules:
  0.0 87.6 jit_solution(16100700144058928261)
XLA Ops:
  0.6 0.0 copy-start.2
  0.6 0.0 copy-start.4
  0.7 0.0 copy-start
  0.7 0.0 copy-start.1
  0.7 0.0 copy-start.3
  0.7 0.6 copy-done.2
  1.3 0.0 copy-done.4
  1.3 0.0 copy-done
  1.3 0.0 copy-done.1
  1.4 0.0 copy-done.3
  1.4 84.3 %shard_map.112 = (bf16[128,256]{1,0:T(8,128)(2,1)S(1)}, f32[2,128]{1,0:T(2,128)S(1)}, f32[256,128]{1,0:T(8,128)S(1)}) custom-call(bf16[128,2304]{1,0:T(8,128)(2,1)} %main_query.1, bf16[576,256]{1,0:T(8,128)(2,1)} %bitcast.13, f32[4,128]{1,0:T(4,128)S(1)} %bitcast.7, bf16[128,256]{1,0:T(8,128)(2,1)} %index_query.1, f32[2,128]{1,0:T(2,128)S(1)} %bitcast.8, ...), custom_call_target="tpu_custom_call" | custom-call | tf_op jit(solution)/shard_map/pallas_call | solution.py:567
  85.7 0.6 copy.15
  86.3 0.6 copy.16
  86.9 0.7 copy.17
Async XLA Ops:
  0.6 0.7 copy-start.2
  0.6 0.7 copy-start.4
  0.7 0.7 copy-start
  0.7 0.7 copy-start.1
  0.7 0.7 copy-start.3

commit v3 on v2

--- a/solution.py
+++ b/solution.py
@@ -64,6 +64,10 @@
     narrow_query,
     wide_query,
     scores,
+    peaks,
+    sums,
+    index_score,
+    dscores,
     ask_out,
     ask_in,
     mass_out,
@@ -73,15 +77,14 @@
     act,
     upper,
     lower,
-    rest_weight,
     terms_out,
     terms_in,
+    shared,
     back_out,
     back_in,
     part_out,
     part_in,
     final,
-    wide_grad,
     weight_grad,
     local_sem,
     cross_send,
@@ -96,6 +99,8 @@
     mass_sem,
     terms_sem,
     back_sem,
+    shared_send,
+    shared_recv,
     part_send,
     part_recv,
     final_sem,
@@ -144,42 +149,6 @@
                 barrier, inc=1, device_id={"seq": lax.rem(other, ns)}, device_id_type=MESH
             )
     lax.fori_loop(1, nh, greet, 0)
-
-    low = lax.broadcasted_iota(jnp.int32, (8, 128), 0) < 4
-    lane = lax.broadcasted_iota(jnp.int32, (8, 128), 1)
-    rows[...] = jnp.zeros_like(rows)
-    rows[0:4, :] = outside[...]
-    rows[4:6, :] = index_weights[...]
-    rows[6:7, :] = query_pos[...].astype(F32)
-    rows[7:8, :] = index_outside[...]
-    cols[...] = rows[...].T
-    for k in range(STEPS):
-        here = jnp.where(seq >= STEPS - 1 - k, 0.0, ABSENT)
-        own = key_pos[...].astype(F32) if k == STEPS - 1 else jnp.zeros((1, kb), F32)
-        place[:, k * kb : (k + 1) * kb] = own + here
-        lat[k, 0:PAD, :] = jnp.zeros((PAD, kb), BF16)
-        lat[k, PAD + WIDTH : PAD + WIDTH + PAD, :] = jnp.zeros((PAD, kb), BF16)
-    local[6].wait()
-    wide_query[...] = narrow_query[...].astype(F32)
-
-    def ask(c, carry):
-        at = pl.ds(pl.multiple_of(8 * c, 8), 8)
-        values = wide_query[at, :]
-        column = cols[at, :]
-        first = jnp.broadcast_to(column[:, 4:5], (8, 128))
-        second = jnp.broadcast_to(column[:, 5:6], (8, 128))
-        pair = split_pair(values[:, :IDIM], values[:, IDIM:], low)
-        weights = split_pair(first, second, low)
-        for i in range(2):
-            weight = weights[i]
-            top = high_part(weight)
-            mid = high_part(weight - top)
-            end = weight - top - mid
-            packed = jnp.where(lane == 0, top, jnp.where(lane == 1, mid, end))
-            ask_out[2 * c + i] = jnp.concatenate([pair[i], packed], 0).astype(BF16)
-        return carry
-
-    lax.fori_loop(0, chunks, ask, 0)
 
     pl.semaphore_wait(barrier, nh - 1 + 2 * (STEPS - 1))
 
@@ -245,6 +214,54 @@
             device_id_type=MESH,
         )
 
+    def all_of(source, target, sems):
+        return exchange(
+            source.at[pl.ds(0, nh - 1)], target.at[pl.ds(0, nh - 1)], sems, lax.rem(head + 1, nh), 0
+        )
+
+    low = lax.broadcasted_iota(jnp.int32, (8, 128), 0) < 4
+    lane = lax.broadcasted_iota(jnp.int32, (8, 128), 1)
+    rows[...] = jnp.zeros_like(rows)
+    rows[0:4, :] = outside[...]
+    rows[4:6, :] = index_weights[...]
+    rows[6:7, :] = query_pos[...].astype(F32)
+    rows[7:8, :] = index_outside[...]
+    cols[...] = rows[...].T
+    for k in range(STEPS):
+        here = jnp.where(seq >= STEPS - 1 - k, 0.0, ABSENT)
+        own = key_pos[...].astype(F32) if k == STEPS - 1 else jnp.zeros((1, kb), F32)
+        place[:, k * kb : (k + 1) * kb] = own + here
+        lat[k, 0:PAD, :] = jnp.zeros((PAD, kb), BF16)
+        lat[k, PAD + WIDTH : PAD + WIDTH + PAD, :] = jnp.zeros((PAD, kb), BF16)
+    wide_lane = lax.broadcasted_iota(jnp.int32, (q_rows, 128), 1)
+    for parity in range(2):
+        for i in range(2):
+            at = slice(i * q_rows, (i + 1) * q_rows)
+            h = 2 * i + parity
+            peaks[parity, at, :] = jnp.where(wide_lane == STEPS, cols[:, h : h + 1], NEGATIVE)
+            sums[parity, at, :] = jnp.where(wide_lane == STEPS, 1.0, 0.0)
+    local[6].wait()
+    wide_query[...] = narrow_query[...].astype(F32)
+
+    def ask(c, carry):
+        at = pl.ds(pl.multiple_of(8 * c, 8), 8)
+        values = wide_query[at, :]
+        column = cols[at, :]
+        first = jnp.broadcast_to(column[:, 4:5], (8, 128))
+        second = jnp.broadcast_to(column[:, 5:6], (8, 128))
+        pair = split_pair(values[:, :IDIM], values[:, IDIM:], low)
+        weights = split_pair(first, second, low)
+        for i in range(2):
+            weight = weights[i]
+            top = high_part(weight)
+            mid = high_part(weight - top)
+            end = weight - top - mid
+            packed = jnp.where(lane == 0, top, jnp.where(lane == 1, mid, end))
+            ask_out[2 * c + i] = jnp.concatenate([pair[i], packed], 0).astype(BF16)
+        return carry
+
+    lax.fori_loop(0, chunks, ask, 0)
+
     def send_ask(r, carry):
         peer = lax.rem(head + r, nh)
         exchange(ask_out.at[peer], ask_in.at[nh - 1 - r], ask_sem, peer, 0).start()
@@ -253,20 +270,29 @@
     lax.fori_loop(1, nh, send_ask, 0)
     ask_in[nh - 1] = ask_out[head]
 
-    def all_of(source, target, sems):
-        return exchange(
-            source.at[pl.ds(0, nh - 1)], target.at[pl.ds(0, nh - 1)], sems, lax.rem(head + 1, nh), 0
-        )
-
     def score_block(k):
         at = pl.ds(pl.multiple_of(k * kb, 128), kb)
+        visible = place[:, at] <= cols[:, 6:7]
         for parity in range(2):
             table = lat[k, PAD * (1 - parity) : PAD * (1 - parity) + WIDE, :]
-            scores[parity, :, at] = dot(queries[parity], table, ((1,), (0,))) * SCORE_SCALE
+            x = dot(queries[parity], table, ((1,), (0,))) * SCORE_SCALE
+            for i in range(2):
+                own = slice(i * q_rows, (i + 1) * q_rows)
+                masked = jnp.where(visible, x[own, :], NEGATIVE)
+                peak = jnp.max(masked, axis=1, keepdims=True)
+                e = jnp.exp(masked - peak)
+                scores[parity, own, at] = e
+                total = jnp.sum(e, axis=1, keepdims=True)
+                peaks[parity, own, :] = jnp.where(wide_lane == k, peak, peaks[parity, own, :])
+                sums[parity, own, :] = jnp.where(wide_lane == k, total, sums[parity, own, :])
 
     def act_block(k, asked):
         at = pl.ds(pl.multiple_of(k * kb, 128), kb)
-        act[:, at] = dot(asked, keys[k], ((1,), (1,))) * FACTOR
+        a = dot(asked, keys[k], ((1,), (1,))) * FACTOR
+        act[:, at] = a
+        weight = near_weight[...]
+        weighed = jnp.concatenate([weight] * blocks, 1) * jnp.maximum(a, 0.0)
+        index_score[:, at] = jnp.sum(weighed.reshape(nh, 8, kb), axis=0)
 
     def to_head(part, i, peer):
         return pltpu.make_async_remote_copy(
@@ -323,42 +349,30 @@
         forward[i].start()
     score_block(1)
 
-    all_of(ask_out, ask_in, ask_sem).wait_recv()
-
-    def unpack(g, carry):
-        at = pl.ds(pl.multiple_of(8 * g, 8), 8)
-        both = ask_in[g].astype(F32)
-        near_query[at, :] = both[0:8, :]
-        packed = both[8:16, :]
-        weight = packed[:, 0:1] + (packed[:, 1:2] + packed[:, 2:3])
-        near_weight[at, :] = jnp.broadcast_to(weight, (8, 128))
-        return carry
-
-    lax.fori_loop(0, nh, unpack, 0)
-    asked = near_query[...].astype(BF16)
-    act_block(STEPS - 1, asked)
-    act_block(early, asked)
-    act_block(1, asked)
+
     forward[1].wait_recv()
     forward[2].wait_recv()
     score_block(late)
 
+    for parity in range(2):
+        peak = peaks[parity]
+        share = jnp.exp(peak - jnp.max(peak, axis=1, keepdims=True))
+        total = jnp.sum(share * sums[parity], axis=1, keepdims=True)
+        peaks[parity] = share * (1.0 / total)
+
     def soften(step, carry):
         c = lax.rem(step + head // 2 + 1, chunks)
-        at = pl.ds(pl.multiple_of(8 * c, 8), 8)
-        column = cols[at, :]
-        visible = place[...] <= column[:, 6:7]
-        mass = jnp.zeros((8, window), F32)
-        for parity in range(2):
-            for i in range(2):
-                h = 2 * i + parity
-                from_row = pl.multiple_of(i * q_rows + 8 * c, 8)
-                x = jnp.where(visible, scores[parity, pl.ds(from_row, 8), :], NEGATIVE)
-                out = column[:, h : h + 1]
-                top = jnp.maximum(jnp.max(x, axis=1, keepdims=True), out)
-                e = jnp.exp(x - top)
-                total = jnp.sum(e, axis=1, keepdims=True) + jnp.exp(out - top)
-                mass = mass + e * (1.0 / total)
+        parts = []
+        for k in range(STEPS):
+            part = jnp.zeros((8, kb), F32)
+            for parity in range(2):
+                for i in range(2):
+                    own = pl.ds(pl.multiple_of(i * q_rows + 8 * c, 8), 8)
+                    part = part + (
+                        scores[parity, own, k * kb : (k + 1) * kb] * peaks[parity, own, k : k + 1]
+                    )
+            parts.append(part)
+        mass = jnp.concatenate(parts, 1)
         halves = split_pair(
             mass[:, :half], mass[:, half:], lax.broadcasted_iota(jnp.int32, (8, half), 0) < 4
         )
@@ -378,14 +392,21 @@
     lax.fori_loop(0, chunks, soften, 0)
     mass_in[nh - 1] = mass_out[head]
 
+    all_of(ask_out, ask_in, ask_sem).wait_recv()
+
+    both = ask_in[...].astype(F32)
+    near_query[...] = both[:, 0:8, :].reshape(8 * nh, 128)
+    packed = both[:, 8:16, :].reshape(8 * nh, 128)
+    weight = packed[:, 0:1] + (packed[:, 1:2] + packed[:, 2:3])
+    near_weight[...] = jnp.broadcast_to(weight, (8 * nh, 128))
+    asked = near_query[...].astype(BF16)
+    act_block(STEPS - 1, asked)
+    act_block(early, asked)
+    act_block(1, asked)
     forward[0].wait_recv()
     act_block(late, asked)
 
-    def add_score(g, total):
-        at = pl.ds(pl.multiple_of(8 * g, 8), 8)
-        return total + near_weight[at, 0:1] * jnp.maximum(act[at, :], 0.0)
-
-    score = lax.fori_loop(0, nh, add_score, jnp.zeros((8, window), F32))
+    score = index_score[...]
     score = score + swap(score)
     odd = lax.rem(head, 2)
     column = cols[pl.ds(pl.multiple_of(8 * (head // 2), 8), 8), :]
@@ -416,57 +437,140 @@
     target = mass * (1.0 / jnp.sum(mass, axis=1, keepdims=True))
     dscore = (predicted - target) * float(window)
     d_high = high_part(dscore)
-    d_low = dscore - d_high
-
-    def gate(g, carry):
-        at = pl.ds(pl.multiple_of(16 * g, 16), 16)
-        a = act[at, :]
-        on = a > 0.0
-        upper[at, :] = jnp.where(on, jnp.concatenate([d_high, d_high], 0), 0.0).astype(BF16)
-        lower[at, :] = jnp.where(on, jnp.concatenate([d_low, d_low], 0), 0.0).astype(BF16)
-        share = jnp.sum(
-            jnp.concatenate([dscore, dscore], 0) * jnp.maximum(a, 0.0), axis=1, keepdims=True
-        )
-        rest_weight[at, :] = jnp.broadcast_to(share, (16, 128))
-        return carry
-
-    lax.fori_loop(0, nh // 2, gate, 0)
-
-    for k in range(STEPS):
-        at = slice(k * kb, (k + 1) * kb)
-        high_block = upper[:, at]
-        terms = dot(turned_high, high_block, ((1,), (0,)))
-        terms = terms + dot(turned_low, high_block, ((1,), (0,)))
-        terms = terms + dot(turned_high, lower[:, at], ((1,), (0,)))
+    dscores[0] = d_high
+    dscores[1] = dscore - d_high
+
+    def term_block(k):
+        at = pl.ds(pl.multiple_of(k * kb, 128), kb)
+        on = act[:, at].reshape(nh, 8, kb) > 0.0
+        gated = []
+        for i in range(2):
+            chosen = jnp.where(on, dscores[i, :, at][None], 0.0)
+            gated.append(chosen.reshape(8 * nh, kb).astype(BF16))
+        upper[:, at] = gated[0]
+        lower[:, at] = gated[1]
+        terms = dot(turned_high, gated[0], ((1,), (0,)))
+        terms = terms + dot(turned_low, gated[0], ((1,), (0,)))
+        terms = terms + dot(turned_high, gated[1], ((1,), (0,)))
         terms = terms * FACTOR
         for tile in range(tiles):
             d, b = tile // blocks, tile % blocks
-            terms_out[tile // per, k, tile % per] = terms[
+            terms_out[k, tile // per, tile % per] = terms[
                 8 * d : 8 * d + 8, 128 * b : 128 * b + 128
             ]
 
-    def send_terms(r, carry):
-        peer = lax.rem(head + r, nh)
-        exchange(terms_out.at[peer], terms_in.at[nh - 1 - r], terms_sem, peer, 0).start()
-        return carry
-
-    lax.fori_loop(1, nh, send_terms, 0)
-    terms_in[nh - 1] = terms_out[head]
+    term_block(3 - 3 * core)
+    share_first = to_seq(
+        terms_out.at[3 - 3 * core], shared.at[0], shared_send, shared_recv, 0, sibling
+    )
+    share_second = to_seq(terms_out.at[1], shared.at[1], shared_send, shared_recv, 1, sibling)
+    share_first.start()
+    term_block(core)
+
+    @pl.when(core == 1)
+    def _():
+        share_second.start()
+
+    term_block(1 + core)
+    term_block(2 + core)
+    share_first.wait_recv()
+
+    @pl.when(core == 0)
+    def _():
+        share_second.wait_recv()
+        terms_out[1] = terms_out[1] + shared[0]
+        terms_out[2] = terms_out[2] + shared[1]
+
+    @pl.when(core == 1)
+    def _():
+        terms_out[2] = terms_out[2] + shared[0]
+
+    def terms_to(first, count, peer, slot):
+        return exchange(
+            terms_out.at[pl.ds(first, count), peer],
+            terms_in.at[pl.ds(first, count), slot],
+            terms_sem, peer, 0,
+        )
+
+    def terms_all(first, count):
+        return exchange(
+            terms_out.at[pl.ds(first, count), pl.ds(0, nh - 1)],
+            terms_in.at[pl.ds(first, count), pl.ds(0, nh - 1)],
+            terms_sem, lax.rem(head + 1, nh), 0,
+        )
+
+    def send_terms(first, count):
+        def send(r, carry):
+            terms_to(first, count, lax.rem(head + r, nh), nh - 1 - r).start()
+            return carry
+
+        lax.fori_loop(1, nh, send, 0)
+
+    @pl.when(core == 0)
+    def _():
+        send_terms(0, 3)
+
+    @pl.when(core == 1)
+    def _():
+        send_terms(2, 2)
 
     all_keys = keys[...].reshape(window, IDIM)
     near_grad = dot(upper[...], all_keys, ((1,), (0,))) + dot(lower[...], all_keys, ((1,), (0,)))
-    wide_grad[...] = near_grad * FACTOR * near_weight[...]
-
-    def pack_back(g, carry):
-        at = pl.ds(pl.multiple_of(8 * g, 8), 8)
-        share = rest_weight[at, :]
-        top = high_part(share)
-        mid = high_part(share - top)
-        packed = jnp.where(lane == 0, top, jnp.where(lane == 1, mid, share - top - mid))
-        back_out[g] = jnp.concatenate([wide_grad[at, :], packed], 0).astype(BF16)
-        return carry
-
-    lax.fori_loop(0, nh, pack_back, 0)
+    near_grad = near_grad * FACTOR * near_weight[...]
+
+    share = jnp.zeros((8 * nh, 1), F32)
+    for k in range(STEPS):
+        at = slice(k * kb, (k + 1) * kb)
+        rectified = jnp.maximum(act[:, at], 0.0).reshape(nh, 8, kb)
+        product = (rectified * dscore[:, at][None]).reshape(8 * nh, kb)
+        share = share + jnp.sum(product, axis=1, keepdims=True)
+    tall_lane = lax.broadcasted_iota(jnp.int32, (8 * nh, 128), 1)
+    top = high_part(share)
+    mid = high_part(share - top)
+    packed = jnp.where(tall_lane == 0, top, jnp.where(tall_lane == 1, mid, share - top - mid))
+    back_out[...] = jnp.concatenate(
+        [near_grad.reshape(nh, 8, 128), packed.reshape(nh, 8, 128)], 1
+    ).astype(BF16)
+
+    def sum_terms(k):
+        total = terms_out[k, head]
+        for g in range(nh - 1):
+            total = total + terms_in[k, g]
+        part_out[k] = total
+
+    behind = lax.rem(seq + ns - 2, ns)
+
+    def part(k, slot, other):
+        return pltpu.make_async_remote_copy(
+            src_ref=part_out.at[k],
+            dst_ref=part_in.at[slot],
+            send_sem=part_send.at[k],
+            recv_sem=part_recv.at[slot],
+            device_id={"seq": other},
+            device_id_type=MESH,
+        )
+
+    part_even = [
+        part(1, 1, behind),
+        part(2, 0, lax.rem(seq + ns - 1, ns)),
+        part(0, 1, lax.rem(seq + ns - 3, ns)),
+    ]
+    part_odd = part(2, 0, sibling)
+
+    @pl.when(core == 0)
+    def _():
+        terms_all(0, 3).wait_recv()
+        for k in (1, 2, 0):
+            sum_terms(k)
+        for copy in part_even:
+            copy.start()
+
+    @pl.when(core == 1)
+    def _():
+        terms_all(2, 2).wait_recv()
+        for k in (2, 3):
+            sum_terms(k)
+        part_odd.start()
 
     def send_back(r, carry):
         peer = lax.rem(head + r, nh)
@@ -476,29 +580,9 @@
     lax.fori_loop(1, nh, send_back, 0)
     back_in[head] = back_out[nh - 1]
 
-    all_of(terms_out, terms_in, terms_sem).wait_recv()
-    summed = terms_in[0]
-    for g in range(1, nh):
-        summed = summed + terms_in[g]
-    part_out[...] = summed
-    part_copies = []
-    for k in range(STEPS - 1):
-        distance = STEPS - 1 - k
-        copy = pltpu.make_async_remote_copy(
-            src_ref=part_out.at[k],
-            dst_ref=part_in.at[k],
-            send_sem=part_send.at[k],
-            recv_sem=part_recv.at[k],
-            device_id={"seq": lax.rem(seq + ns - distance, ns)},
-            device_id_type=MESH,
-        )
-        copy.start()
-        part_copies.append(copy)
-    mine = part_out[STEPS - 1]
-    for copy in part_copies:
-        copy.wait_recv()
-    for k in range(STEPS - 1):
-        mine = mine + part_in[k]
+    part(1, 0, behind).wait_recv()
+    part(1, 1, behind).wait_recv()
+    mine = jnp.where(core == 1, part_out[3], 0.0) + part_in[0] + part_in[1]
     final[head] = mine
 
     def send_final(r, carry):
@@ -534,11 +618,23 @@
         columns = [final[(d * blocks + b) // per, (d * blocks + b) % per] for d in range(16)]
         grad_keys[128 * b : 128 * b + 128, :] = jnp.concatenate(columns, 0).T
 
-    for copy in crossing + direct + gathered + forward + part_copies:
+    for copy in crossing + direct + gathered + forward + [share_first]:
         copy.wait_send()
+
+    @pl.when(core == 0)
+    def _():
+        terms_all(0, 3).wait_send()
+        for copy in part_even:
+            copy.wait_send()
+
+    @pl.when(core == 1)
+    def _():
+        share_second.wait_send()
+        terms_all(2, 2).wait_send()
+        part_odd.wait_send()
+
     all_of(ask_out, ask_in, ask_sem).wait_send()
     all_of(mass_out, mass_in, mass_sem).wait_send()
-    all_of(terms_out, terms_in, terms_sem).wait_send()
     all_of(back_out, back_in, back_sem).wait_send()
     all_of(final, final, final_sem).wait_send()
 
@@ -583,6 +679,10 @@
                 pltpu.VMEM((q, 2 * IDIM), BF16),
                 pltpu.VMEM((q, 2 * IDIM), F32),
                 pltpu.VMEM((2, 2 * q, window), F32),
+                pltpu.VMEM((2, 2 * q, 128), F32),
+                pltpu.VMEM((2, 2 * q, 128), F32),
+                pltpu.VMEM((8, window), F32),
+                pltpu.VMEM((2, 8, window), F32),
                 pltpu.VMEM((nh, 16, 128), BF16),
                 pltpu.VMEM((nh, 16, 128), BF16),
                 pltpu.VMEM((nh, 16, window // 4), BF16),
@@ -592,15 +692,14 @@
                 pltpu.VMEM((8 * nh, window), F32),
                 pltpu.VMEM((8 * nh, window), BF16),
                 pltpu.VMEM((8 * nh, window), BF16),
-                pltpu.VMEM((8 * nh, 128), F32),
-                pltpu.VMEM((nh, STEPS, per, 8, 128), F32),
-                pltpu.VMEM((nh, STEPS, per, 8, 128), F32),
+                pltpu.VMEM((STEPS, nh, per, 8, 128), F32),
+                pltpu.VMEM((STEPS, nh, per, 8, 128), F32),
+                pltpu.VMEM((2, nh, per, 8, 128), F32),
                 pltpu.VMEM((nh, 16, 128), BF16),
                 pltpu.VMEM((nh, 16, 128), BF16),
                 pltpu.VMEM((STEPS, per, 8, 128), F32),
-                pltpu.VMEM((STEPS - 1, per, 8, 128), F32),
+                pltpu.VMEM((2, per, 8, 128), F32),
                 pltpu.VMEM((nh, per, 8, 128), F32),
-                pltpu.VMEM((8 * nh, 128), F32),
                 pltpu.VMEM((q, 128), F32),
                 dma((7,)),
                 dma((3,)),
@@ -615,8 +714,10 @@
                 dma((2,)),
                 dma((2,)),
                 dma((2,)),
+                dma((2,)),
+                dma((2,)),
                 dma((STEPS - 1,)),
-                dma((STEPS - 1,)),
+                dma((2,)),
                 dma((2,)),
             ],
             compiler_params=pltpu.CompilerParams(

time: 87.7 us -> 74.8 us (0.85)
  Pallas kernels: 84.3 us -> 71.4 us
    pallas_call x1, Pallas kernels: 84.3 us -> 71.4 us  [shards(): pl.pallas_call(functools.partial(kernel, ns, nh), out_shape=(jax.ShapeDty...]
where the time goes in v3:
time: 74.8 us; the launch traced here: 74.7 us
  Pallas kernels  71.4 us (95%)
  local copies, waits for them, and re-layouts  2.54 us (3%)
    pallas_call x1, Pallas kernels, shards(): pl.pallas_call(functools.partial(kernel, ns, nh), out_shape=(jax.ShapeDty...  71.4 us
    unnamed x13, local copies, waits for them, and re-layouts  2.54 us

profile of v3, /device:TPU:1, one launch (start us, length us, event | category | flops | bytes accessed | tf_op | source)
XLA Modules:
  0.0 74.7 jit_solution(4018781181661619561)
XLA Ops:
  0.6 0.0 copy-start.2
  0.6 0.0 copy-start.4
  0.7 0.0 copy-start
  0.7 0.0 copy-start.1
  0.7 0.0 copy-start.3
  0.7 0.6 copy-done.2
  1.3 0.0 copy-done.4
  1.3 0.0 copy-done
  1.3 0.0 copy-done.1
  1.4 0.0 copy-done.3
  1.4 71.4 %shard_map.112 = (bf16[128,256]{1,0:T(8,128)(2,1)S(1)}, f32[2,128]{1,0:T(2,128)S(1)}, f32[256,128]{1,0:T(8,128)S(1)}) custom-call(bf16[128,2304]{1,0:T(8,128)(2,1)} %main_query.1, bf16[576,256]{1,0:T(8,128)(2,1)} %bitcast.13, f32[4,128]{1,0:T(4,128)S(1)} %bitcast.7, bf16[128,256]{1,0:T(8,128)(2,1)} %index_query.1, f32[2,128]{1,0:T(2,128)S(1)} %bitcast.8, ...), custom_call_target="tpu_custom_call" | custom-call | tf_op jit(solution)/shard_map/pallas_call | solution.py:663
  72.8 0.6 copy.15
  73.4 0.6 copy.16
  74.0 0.7 copy.17
Async XLA Ops:
  0.6 0.7 copy-start.2
  0.6 0.7 copy-start.4
  0.7 0.7 copy-start
  0.7 0.7 copy-start.1
  0.7 0.7 copy-start.3

commit v4 on v3

--- a/solution.py
+++ b/solution.py
@@ -45,16 +45,21 @@
     nh,
     main_query,
     latent,
+    far_outside,
+    index_query,
+    far_weights,
+    index_keys,
+    far_limit,
+    far_query_pos,
+    far_key_pos,
+    grad_query,
+    grad_weight,
+    grad_keys,
     outside,
-    index_query,
     index_weights,
-    index_keys,
     index_outside,
     query_pos,
     key_pos,
-    grad_query,
-    grad_weight,
-    grad_keys,
     rows,
     cols,
     place,
@@ -86,6 +91,7 @@
     part_in,
     final,
     weight_grad,
+    small_sem,
     local_sem,
     cross_send,
     cross_recv,
@@ -98,6 +104,7 @@
     ask_sem,
     mass_sem,
     terms_sem,
+    alone_sem,
     back_sem,
     shared_send,
     shared_recv,
@@ -132,7 +139,19 @@
     )
     local.append(pltpu.make_async_copy(index_keys, keys.at[STEPS - 1], local_sem.at[5]))
     local.append(pltpu.make_async_copy(index_query, narrow_query, local_sem.at[6]))
-    for copy in local:
+    small = [
+        pltpu.make_async_copy(source, target, small_sem.at[i])
+        for i, (source, target) in enumerate(
+            (
+                (far_outside, outside),
+                (far_weights, index_weights),
+                (far_limit, index_outside),
+                (far_query_pos, query_pos),
+                (far_key_pos, key_pos),
+            )
+        )
+    ]
+    for copy in small + local[6:] + local[:6]:
         copy.start()
 
     barrier = pltpu.get_barrier_semaphore()
@@ -201,7 +220,7 @@
         to_seq(index_keys, keys.at[late], direct_send, direct_recv, 0, onward),
         to_seq(latent, lat_rows(late, 0, WIDTH), direct_send, direct_recv, 1, onward),
     ]
-    for copy in crossing + direct:
+    for copy in crossing[::-1] + direct[::-1]:
         copy.start()
 
     def exchange(source, target, sems, peer, slot):
@@ -221,6 +240,8 @@
 
     low = lax.broadcasted_iota(jnp.int32, (8, 128), 0) < 4
     lane = lax.broadcasted_iota(jnp.int32, (8, 128), 1)
+    for copy in small:
+        copy.wait()
     rows[...] = jnp.zeros_like(rows)
     rows[0:4, :] = outside[...]
     rows[4:6, :] = index_weights[...]
@@ -307,22 +328,27 @@
     for copy in local[:6]:
         copy.wait()
     score_block(STEPS - 1)
-    for copy in crossing:
-        copy.wait_recv()
-
-    def push_ring(r, carry):
-        peer = lax.rem(head + r * X_RUN, nh)
-        to_head(key_part(1, key_at, key_rows), 0, peer).start()
-        to_head(lat_rows(1, ring_at, ring_rows), 1, peer).start()
-        return carry
-
     def push_run(r, carry):
         peer = ring * X_RUN + lax.rem(run + r, X_RUN)
         to_head(lat_rows(1, run_at, run_rows), 2, peer).start()
         return carry
 
+    def push_ring(r, carry):
+        peer = lax.rem(head + r * X_RUN, nh)
+        to_head(lat_rows(1, ring_at, ring_rows), 1, peer).start()
+        return carry
+
+    def push_keys(r, carry):
+        peer = lax.rem(head + r * X_RUN, nh)
+        to_head(key_part(1, key_at, key_rows), 0, peer).start()
+        return carry
+
+    crossing[2].wait_recv()
+    lax.fori_loop(1, X_RUN, push_run, 0)
+    crossing[1].wait_recv()
     lax.fori_loop(1, rings, push_ring, 0)
-    lax.fori_loop(1, X_RUN, push_run, 0)
+    crossing[0].wait_recv()
+    lax.fori_loop(1, rings, push_keys, 0)
     gathered = [
         to_head(key_part(1, 0, key_rows * (rings - 1)), 0, head),
         to_head(lat_rows(1, 0, ring_rows * (rings - 1)), 1, head),
@@ -344,10 +370,12 @@
     for copy in direct:
         copy.wait_recv()
     score_block(early)
-    for i in range(3):
+    for i in (2, 1):
         gathered[i].wait_recv()
         forward[i].start()
     score_block(1)
+    gathered[0].wait_recv()
+    forward[0].start()
 
 
     forward[1].wait_recv()
@@ -459,6 +487,27 @@
                 8 * d : 8 * d + 8, 128 * b : 128 * b + 128
             ]
 
+    def terms_to(first, count, peer, slot, sems):
+        return exchange(
+            terms_out.at[pl.ds(first, count), peer],
+            terms_in.at[pl.ds(first, count), slot],
+            sems, peer, 0,
+        )
+
+    def terms_all(first, count, sems):
+        return exchange(
+            terms_out.at[pl.ds(first, count), pl.ds(0, nh - 1)],
+            terms_in.at[pl.ds(first, count), pl.ds(0, nh - 1)],
+            sems, lax.rem(head + 1, nh), 0,
+        )
+
+    def send_terms(first, count, sems):
+        def send(r, carry):
+            terms_to(first, count, lax.rem(head + r, nh), nh - 1 - r, sems).start()
+            return carry
+
+        lax.fori_loop(1, nh, send, 0)
+
     term_block(3 - 3 * core)
     share_first = to_seq(
         terms_out.at[3 - 3 * core], shared.at[0], shared_send, shared_recv, 0, sibling
@@ -471,8 +520,9 @@
     def _():
         share_second.start()
 
-    term_block(1 + core)
-    term_block(2 + core)
+    term_block(1 + 2 * core)
+    send_terms(3 * core, 1, alone_sem)
+    term_block(2)
     share_first.wait_recv()
 
     @pl.when(core == 0)
@@ -480,39 +530,12 @@
         share_second.wait_recv()
         terms_out[1] = terms_out[1] + shared[0]
         terms_out[2] = terms_out[2] + shared[1]
+        send_terms(1, 2, terms_sem)
 
     @pl.when(core == 1)
     def _():
         terms_out[2] = terms_out[2] + shared[0]
-
-    def terms_to(first, count, peer, slot):
-        return exchange(
-            terms_out.at[pl.ds(first, count), peer],
-            terms_in.at[pl.ds(first, count), slot],
-            terms_sem, peer, 0,
-        )
-
-    def terms_all(first, count):
-        return exchange(
-            terms_out.at[pl.ds(first, count), pl.ds(0, nh - 1)],
-            terms_in.at[pl.ds(first, count), pl.ds(0, nh - 1)],
-            terms_sem, lax.rem(head + 1, nh), 0,
-        )
-
-    def send_terms(first, count):
-        def send(r, carry):
-            terms_to(first, count, lax.rem(head + r, nh), nh - 1 - r).start()
-            return carry
-
-        lax.fori_loop(1, nh, send, 0)
-
-    @pl.when(core == 0)
-    def _():
-        send_terms(0, 3)
-
-    @pl.when(core == 1)
-    def _():
-        send_terms(2, 2)
+        send_terms(2, 1, terms_sem)
 
     all_keys = keys[...].reshape(window, IDIM)
     near_grad = dot(upper[...], all_keys, ((1,), (0,))) + dot(lower[...], all_keys, ((1,), (0,)))
@@ -559,17 +582,20 @@
 
     @pl.when(core == 0)
     def _():
-        terms_all(0, 3).wait_recv()
-        for k in (1, 2, 0):
+        terms_all(0, 1, alone_sem).wait_recv()
+        sum_terms(0)
+        terms_all(1, 2, terms_sem).wait_recv()
+        for k in (1, 2):
             sum_terms(k)
         for copy in part_even:
             copy.start()
 
     @pl.when(core == 1)
     def _():
-        terms_all(2, 2).wait_recv()
-        for k in (2, 3):
-            sum_terms(k)
+        terms_all(3, 1, alone_sem).wait_recv()
+        sum_terms(3)
+        terms_all(2, 1, terms_sem).wait_recv()
+        sum_terms(2)
         part_odd.start()
 
     def send_back(r, carry):
@@ -623,14 +649,16 @@
 
     @pl.when(core == 0)
     def _():
-        terms_all(0, 3).wait_send()
+        terms_all(0, 1, alone_sem).wait_send()
+        terms_all(1, 2, terms_sem).wait_send()
         for copy in part_even:
             copy.wait_send()
 
     @pl.when(core == 1)
     def _():
         share_second.wait_send()
-        terms_all(2, 2).wait_send()
+        terms_all(3, 1, alone_sem).wait_send()
+        terms_all(2, 1, terms_sem).wait_send()
         part_odd.wait_send()
 
     all_of(ask_out, ask_in, ask_sem).wait_send()
@@ -667,9 +695,14 @@
                 jax.ShapeDtypeStruct((2, q), F32),
                 jax.ShapeDtypeStruct((kb, IDIM), F32),
             ),
-            in_specs=[whole, whole, vmem, whole, vmem, whole, vmem, vmem, vmem],
+            in_specs=[whole] * 9,
             out_specs=(vmem, vmem, vmem),
             scratch_shapes=[
+                pltpu.VMEM((4, q), F32),
+                pltpu.VMEM((2, q), F32),
+                pltpu.VMEM((1, q), F32),
+                pltpu.VMEM((1, q), jnp.int32),
+                pltpu.VMEM((1, kb), jnp.int32),
                 pltpu.VMEM((128, q), F32),
                 pltpu.VMEM((q, 128), F32),
                 pltpu.VMEM((1, window), F32),
@@ -701,6 +734,7 @@
                 pltpu.VMEM((2, per, 8, 128), F32),
                 pltpu.VMEM((nh, per, 8, 128), F32),
                 pltpu.VMEM((q, 128), F32),
+                dma((5,)),
                 dma((7,)),
                 dma((3,)),
                 dma((3,)),
@@ -710,6 +744,7 @@
                 dma((3,)),
                 dma((3,)),
                 dma((3,)),
+                dma((2,)),
                 dma((2,)),
                 dma((2,)),
                 dma((2,)),
@@ -724,15 +759,20 @@
                 collective_id=0, has_side_effects=True, vmem_limit_bytes=48 << 20
             ),
         )(
-            pltpu.with_memory_space_constraint(main_query, pltpu.MemorySpace.HBM),
-            pltpu.with_memory_space_constraint(latent.T, pltpu.MemorySpace.HBM),
-            main_outside.T,
-            pltpu.with_memory_space_constraint(index_query, pltpu.MemorySpace.HBM),
-            index_weights.T,
-            pltpu.with_memory_space_constraint(index_keys, pltpu.MemorySpace.HBM),
-            index_outside.reshape(1, q),
-            query_pos.reshape(1, q),
-            key_pos.reshape(1, kb),
+            *(
+                pltpu.with_memory_space_constraint(x, pltpu.MemorySpace.HBM)
+                for x in (
+                    main_query,
+                    latent.T,
+                    main_outside.T,
+                    index_query,
+                    index_weights.T,
+                    index_keys,
+                    index_outside.reshape(1, q),
+                    query_pos.reshape(1, q),
+                    key_pos.reshape(1, kb),
+                )
+            )
         )
         return grad_query, grad_weight.T, grad_keys
 

time: 74.8 us -> 73 us (0.976)
  Pallas kernels: 71.4 us -> 70.4 us
    pallas_call x1, Pallas kernels: 71.4 us -> 70.4 us  [shards(): pl.pallas_call(functools.partial(kernel, ns, nh), out_shape=(jax.ShapeDty...]
    unnamed x13 -> x3, local copies, waits for them, and re-layouts: 2.54 us -> 1.85 us
where the time goes in v4:
time: 73 us; the launch traced here: 72.9 us
  Pallas kernels  70.4 us (96%)
  local copies, waits for them, and re-layouts  1.85 us (3%)
    pallas_call x1, Pallas kernels, shards(): pl.pallas_call(functools.partial(kernel, ns, nh), out_shape=(jax.ShapeDty...  70.4 us
    unnamed x3, local copies, waits for them, and re-layouts  1.85 us

profile of v4, /device:TPU:1, one launch (start us, length us, event | category | flops | bytes accessed | tf_op | source)
XLA Modules:
  0.0 72.9 jit_solution(209195972097197279)
XLA Ops:
  0.6 70.4 %shard_map.112 = (bf16[128,256]{1,0:T(8,128)(2,1)S(1)}, f32[2,128]{1,0:T(2,128)S(1)}, f32[256,128]{1,0:T(8,128)S(1)}) custom-call(bf16[128,2304]{1,0:T(8,128)(2,1)} %main_query.1, bf16[576,256]{1,0:T(8,128)(2,1)} %bitcast.8, f32[4,128]{1,0:T(4,128)} %bitcast.9, bf16[128,256]{1,0:T(8,128)(2,1)} %index_query.1, f32[2,128]{1,0:T(2,128)} %bitcast.10, ...), custom_call_target="tpu_custom_call" | custom-call | tf_op jit(solution)/shard_map/pallas_call | solution.py:691
  71.0 0.6 copy.15
  71.7 0.6 copy.16
  72.2 0.7 copy.17

commit v5 on v4

--- a/solution.py
+++ b/solution.py
@@ -334,6 +334,8 @@
         return carry
 
     def push_ring(r, carry):
+        r = rings - r
+        r = (r + 1) // 2 + lax.rem(r + 1, 2) * (rings - r)
         peer = lax.rem(head + r * X_RUN, nh)
         to_head(lat_rows(1, ring_at, ring_rows), 1, peer).start()
         return carry
@@ -584,11 +586,11 @@
     def _():
         terms_all(0, 1, alone_sem).wait_recv()
         sum_terms(0)
+        part_even[2].start()
         terms_all(1, 2, terms_sem).wait_recv()
         for k in (1, 2):
             sum_terms(k)
-        for copy in part_even:
-            copy.start()
+            part_even[k - 1].start()
 
     @pl.when(core == 1)
     def _():

time: 73 us -> 72.7 us (level)
  no operation moved by 1% of the time
where the time goes in v5:
time: 72.7 us; the launch traced here: 72.5 us
  Pallas kernels  70 us (96%)
  local copies, waits for them, and re-layouts  1.85 us (3%)
    pallas_call x1, Pallas kernels, shards(): pl.pallas_call(functools.partial(kernel, ns, nh), out_shape=(jax.ShapeDty...  70 us
    unnamed x3, local copies, waits for them, and re-layouts  1.85 us

profile of v5, /device:TPU:1, one launch (start us, length us, event | category | flops | bytes accessed | tf_op | source)
XLA Modules:
  0.0 72.5 jit_solution(13375148145523443612)
XLA Ops:
  0.6 70.0 %shard_map.112 = (bf16[128,256]{1,0:T(8,128)(2,1)S(1)}, f32[2,128]{1,0:T(2,128)S(1)}, f32[256,128]{1,0:T(8,128)S(1)}) custom-call(bf16[128,2304]{1,0:T(8,128)(2,1)} %main_query.1, bf16[576,256]{1,0:T(8,128)(2,1)} %bitcast.8, f32[4,128]{1,0:T(4,128)} %bitcast.9, bf16[128,256]{1,0:T(8,128)(2,1)} %index_query.1, f32[2,128]{1,0:T(2,128)} %bitcast.10, ...), custom_call_target="tpu_custom_call" | custom-call | tf_op jit(solution)/shard_map/pallas_call | solution.py:693
  70.7 0.6 copy.15
  71.3 0.6 copy.16
  71.9 0.7 copy.17
